TPU v7x, 32 devices: a whole 2x2x4 slice. The times are simulated.
32 devices in a mesh: dp: 8 (over y, x, core), tensor: 4 (over z).
Axes of the slice: x: 2, y: 2, z: 4, core: 2. Of those that a mesh axis runs over, the one named last changes fastest.
Arguments:
- inputs: bfloat16 [8, 1024, 2048], P('dp'), may hold values from -6 to 6
- segments: int32 [8, 1024], P('dp'), may hold values from 0 to 3, never falling along the last dimension, each value on 1 to 512 neighbouring positions
- cotangent: bfloat16 [8, 1024, 2048], P('dp'), may hold values from -6 to 6
- w_query: bfloat16 [2048, 2048], P(None, 'tensor'), may hold values from -0.046875 to 0.046875
- w_key: bfloat16 [2048, 2048], P(None, 'tensor'), may hold values from -0.046875 to 0.046875
- w_value: bfloat16 [2048, 2048], P(None, 'tensor'), may hold values from -0.125 to 0.125
- w_out: bfloat16 [2048, 2048], P('tensor'), may hold values from -0.5 to 0.5
- w_gate: bfloat16 [2048, 5120], P(None, 'tensor'), may hold values from -0.125 to 0.125
- w_up: bfloat16 [2048, 5120], P(None, 'tensor'), may hold values from -0.125 to 0.125
- w_down: bfloat16 [5120, 2048], P('tensor'), may hold values from -0.125 to 0.125
- gain_attn: float32 [2048], replicated, may hold values from 0.5 to 1.5
- gain_ffn: float32 [2048], replicated, may hold values from 0.5 to 1.5
- bias_table: float32 [32, 32], P(None, 'tensor'), may hold values from -4 to 4
Outputs:
- output: bfloat16 [8, 1024, 2048], P('dp', 'tensor')
- input_grad: bfloat16 [8, 1024, 2048], P('dp', 'tensor')
- query_grad: float32 [2048, 2048], P(None, 'tensor')
- key_grad: float32 [2048, 2048], P(None, 'tensor')
- value_grad: float32 [2048, 2048], P(None, 'tensor')
- out_grad: float32 [2048, 2048], P('tensor')
- gate_grad: float32 [2048, 5120], P(None, 'tensor')
- up_grad: float32 [2048, 5120], P(None, 'tensor')
- down_grad: float32 [5120, 2048], P('tensor')
- gain_attn_grad: float32 [2048], replicated
- gain_ffn_grad: float32 [2048], replicated
- table_grad: float32 [32, 32], P(None, 'tensor')
Inputs may be any that keep to these rules, and one draw needn't show every extreme that they name: `segments`: each row of 1024 tokens holds 4 documents one after another; document numbers never fall along a row; each document has 1 to 512 tokens and one in every row has exactly 512.
All inputs are finite; a program needn't handle non-finite values.
Results may differ from a plain program's by a relative error of at most 0.024.
Values may be sent and summed in bfloat16 or wider, within the bound.
A program may use at most 320 MiB of HBM per device.

v0:
```python
import jax
import jax.numpy as jnp
from jax import lax
from jax.sharding import PartitionSpec as P

thresholds = (12, 16, 23, 32, 46, 64, 91)
highest = lax.Precision.HIGHEST


def buckets_of(start_row, query_count, length):
    queries = start_row + jnp.arange(query_count, dtype=jnp.int32)
    targets = jnp.arange(length, dtype=jnp.int32)
    offset = targets[None, :] - queries[:, None]
    distance = jnp.abs(offset)
    far_bucket = jnp.full(distance.shape, 8, jnp.int32)
    for bound_value in thresholds:
        far_bucket = far_bucket + (distance >= bound_value).astype(jnp.int32)
    near_bucket = jnp.where(distance < 8, distance, far_bucket)
    return near_bucket + 16 * (offset > 0).astype(jnp.int32)


def bucket_onehot(start_row, query_count, length, bucket_count):
    bucket = buckets_of(start_row, query_count, length).reshape(1, query_count * length)
    labels = jnp.arange(bucket_count, dtype=jnp.int32)[:, None]
    return (bucket == labels).astype(jnp.float32)


def project(left_side, right_side):
    return jnp.dot(left_side, right_side, preferred_element_type=jnp.float32)


def project_back(left_side, right_side):
    return lax.dot_general(
        left_side, right_side, (((1,), (1,)), ((), ())), preferred_element_type=jnp.float32
    )


def weight_term(left_side, right_side):
    return lax.dot_general(
        left_side, right_side, (((0,), (0,)), ((), ())), preferred_element_type=jnp.float32
    )


def norm_scale(signal):
    return lax.rsqrt(jnp.mean(signal * signal, axis=-1, keepdims=True) + 1e-06)


def norm_back(signal, rms_scale, gain_vec, grad_normed):
    grad_hat = grad_normed * gain_vec
    inner_mean = jnp.mean(grad_hat * signal, axis=-1, keepdims=True)
    return rms_scale * (grad_hat - signal * rms_scale * rms_scale * inner_mean)


def gain_term(signal, rms_scale, grad_normed):
    return jnp.sum((grad_normed * signal * rms_scale).reshape(-1, signal.shape[-1]), axis=0)


def score_block(query_block, key_row, bias_block, same_doc):
    raw_scores = jnp.einsum(
        "qhd,khd->hqk", query_block, key_row, preferred_element_type=jnp.float32
    )
    return jnp.where(same_doc[None], raw_scores + bias_block, -1000000000.0)


def shards(
    inputs,
    segments,
    cotangent,
    w_query,
    w_key,
    w_value,
    w_out,
    w_gate,
    w_up,
    w_down,
    gain_attn,
    gain_ffn,
    bias_table,
):
    row_count, length, model_width = inputs.shape
    share_rows = length // lax.axis_size("tensor")
    first_row = lax.axis_index("tensor") * share_rows
    bucket_count, head_count = bias_table.shape
    local_width = w_query.shape[1]
    head_dim = local_width // head_count
    block_rows = min(512, length)
    block_count = length // block_rows
    token_count = row_count * length
    plane = (row_count, length, model_width)

    def take_share(signal):
        return lax.dynamic_slice_in_dim(signal, first_row, share_rows, 1)

    flat_inputs = inputs.reshape(token_count, model_width).astype(jnp.float32)
    scale_attn = norm_scale(flat_inputs)
    normed = (flat_inputs * scale_attn * gain_attn).astype(jnp.bfloat16)
    heads_shape = (row_count, length, head_count, head_dim)
    queries = project(normed, w_query).astype(jnp.bfloat16).reshape(heads_shape)
    key_proj = project(normed, w_key).astype(jnp.bfloat16).reshape(heads_shape)
    value_proj = project(normed, w_value).astype(jnp.bfloat16).reshape(heads_shape)
    table_heads = jnp.transpose(bias_table)
    bias_blocks = []
    for block_index in range(block_count):
        onehot = bucket_onehot(block_index * block_rows, block_rows, length, bucket_count)
        bias_flat = jnp.dot(table_heads, onehot, precision=highest)
        bias_blocks.append(bias_flat.reshape(head_count, block_rows, length))
    row_index = 0
    doc_row = segments[row_index]
    pieces = []
    totals_row = []
    for block_index in range(block_count):
        block_start = block_index * block_rows
        same_doc = doc_row[block_start : block_start + block_rows, None] == doc_row[None, :]
        query_block = queries[row_index, block_start : block_start + block_rows]
        scores = score_block(query_block, key_proj[row_index], bias_blocks[block_index], same_doc)
        row_max = jnp.max(scores, axis=-1, keepdims=True)
        weighted = jnp.exp(scores - row_max)
        row_total = jnp.sum(weighted, axis=-1, keepdims=True)
        softmaxed = (weighted / row_total).astype(jnp.bfloat16)
        totals_row.append(row_max + jnp.log(row_total))
        pieces.append(
            jnp.einsum(
                "hqk,khd->qhd", softmaxed, value_proj[row_index], preferred_element_type=jnp.float32
            ).astype(jnp.bfloat16)
        )
    log_totals = [totals_row]
    mixed_rows = [jnp.concatenate(pieces, axis=0)]
    mixed_heads = jnp.stack(mixed_rows).reshape(token_count, local_width)
    attn_part = project(mixed_heads, w_out)
    attn_total = lax.psum(attn_part.astype(jnp.bfloat16), "tensor").astype(jnp.float32)
    middle = flat_inputs + attn_total
    scale_ffn = norm_scale(middle)
    normed_ffn = (middle * scale_ffn * gain_ffn).astype(jnp.bfloat16)
    gate_pre = project(normed_ffn, w_gate)
    up_pre = project(normed_ffn, w_up)
    hidden = (jax.nn.gelu(gate_pre, approximate=True) * up_pre).astype(jnp.bfloat16)
    ffn_part = project(hidden, w_down)
    ffn_total = lax.psum(ffn_part.astype(jnp.bfloat16), "tensor").astype(jnp.float32)
    output = take_share((middle + ffn_total).reshape(plane)).astype(jnp.bfloat16)
    grad_out = cotangent.reshape(token_count, model_width)
    down_grad = weight_term(hidden, grad_out)
    grad_hidden = project_back(grad_out, w_down)
    normed_again = lax.optimization_barrier(normed_ffn)
    gate_back = project(normed_again, w_gate)
    up_back = project(normed_again, w_up)
    act_value, act_pull = jax.vjp(lambda signal: jax.nn.gelu(signal, approximate=True), gate_back)
    grad_gate = act_pull(grad_hidden * up_back)[0].astype(jnp.bfloat16)
    grad_up = (grad_hidden * act_value).astype(jnp.bfloat16)
    gate_grad = weight_term(normed_ffn, grad_gate)
    up_grad = weight_term(normed_ffn, grad_up)
    norm_ffn_part = project_back(grad_gate, w_gate) + project_back(grad_up, w_up)
    grad_normed_ffn = lax.psum(norm_ffn_part.astype(jnp.bfloat16), "tensor").astype(jnp.float32)
    grad_middle = grad_out.astype(jnp.float32) + norm_back(
        middle, scale_ffn, gain_ffn, grad_normed_ffn
    )
    gain_ffn_part = gain_term(
        take_share(middle.reshape(plane)),
        take_share(scale_ffn.reshape(row_count, length, 1)),
        take_share(grad_normed_ffn.reshape(plane)),
    )
    grad_branch = grad_middle.astype(jnp.bfloat16)
    out_grad = weight_term(mixed_heads, grad_branch)
    grad_mixed = project_back(grad_branch, w_out).astype(jnp.bfloat16).reshape(heads_shape)
    score_sums = [
        jnp.zeros((head_count, block_rows, length), jnp.float32)
        for block_index in range(block_count)
    ]
    row_index = 0
    doc_row = segments[row_index]
    key_row = key_proj[row_index]
    value_row = value_proj[row_index]
    key_sum = jnp.zeros((length, head_count, head_dim), jnp.float32)
    value_sum = jnp.zeros((length, head_count, head_dim), jnp.float32)
    query_pieces = []
    for block_index in range(block_count):
        block_start = block_index * block_rows
        same_doc = doc_row[block_start : block_start + block_rows, None] == doc_row[None, :]
        query_block = queries[row_index, block_start : block_start + block_rows]
        grad_block = grad_mixed[row_index, block_start : block_start + block_rows]
        scores = score_block(query_block, key_row, bias_blocks[block_index], same_doc)
        weights_back = jnp.exp(scores - log_totals[row_index][block_index])
        grad_weights = jnp.einsum(
            "qhd,khd->hqk", grad_block, value_row, preferred_element_type=jnp.float32
        )
        row_delta = jnp.sum(weights_back * grad_weights, axis=-1, keepdims=True)
        grad_scores = weights_back * (grad_weights - row_delta)
        score_sums[block_index] = grad_scores
        scores_low = grad_scores.astype(jnp.bfloat16)
        query_pieces.append(
            jnp.einsum(
                "hqk,khd->qhd", scores_low, key_row, preferred_element_type=jnp.float32
            ).astype(jnp.bfloat16)
        )
        key_sum = key_sum + jnp.einsum(
            "hqk,qhd->khd", scores_low, query_block, preferred_element_type=jnp.float32
        )
        value_sum = value_sum + jnp.einsum(
            "hqk,qhd->khd",
            weights_back.astype(jnp.bfloat16),
            grad_block,
            preferred_element_type=jnp.float32,
        )
    query_rows = [jnp.concatenate(query_pieces, axis=0)]
    key_rows = [key_sum.astype(jnp.bfloat16)]
    value_rows = [value_sum.astype(jnp.bfloat16)]
    grad_query = jnp.stack(query_rows).reshape(token_count, local_width)
    grad_key = jnp.stack(key_rows).reshape(token_count, local_width)
    grad_value = jnp.stack(value_rows).reshape(token_count, local_width)
    table_grad = jnp.zeros((bucket_count, head_count), jnp.float32)
    for block_index in range(block_count):
        onehot = bucket_onehot(block_index * block_rows, block_rows, length, bucket_count)
        table_grad = table_grad + lax.dot_general(
            onehot,
            score_sums[block_index].reshape(head_count, block_rows * length),
            (((1,), (1,)), ((), ())),
            precision=highest,
        )
    query_grad = weight_term(normed, grad_query)
    key_grad = weight_term(normed, grad_key)
    value_grad = weight_term(normed, grad_value)
    norm_attn_part = (
        project_back(grad_query, w_query)
        + project_back(grad_key, w_key)
        + project_back(grad_value, w_value)
    )
    grad_normed_attn = lax.psum(norm_attn_part.astype(jnp.bfloat16), "tensor").astype(jnp.float32)
    grad_input = grad_middle + norm_back(flat_inputs, scale_attn, gain_attn, grad_normed_attn)
    input_grad = take_share(grad_input.reshape(plane)).astype(jnp.bfloat16)
    gain_attn_part = gain_term(
        take_share(flat_inputs.reshape(plane)),
        take_share(scale_attn.reshape(row_count, length, 1)),
        take_share(grad_normed_attn.reshape(plane)),
    )
    gain_attn_grad, gain_ffn_grad = lax.psum((gain_attn_part, gain_ffn_part), ("dp", "tensor"))
    reduced = (
        lax.psum_scatter(
            query_grad.astype(jnp.bfloat16), "dp", scatter_dimension=0, tiled=True
        ).astype(jnp.float32),
        lax.psum_scatter(
            key_grad.astype(jnp.bfloat16), "dp", scatter_dimension=0, tiled=True
        ).astype(jnp.float32),
        lax.psum_scatter(
            value_grad.astype(jnp.bfloat16), "dp", scatter_dimension=0, tiled=True
        ).astype(jnp.float32),
        lax.psum_scatter(
            out_grad.astype(jnp.bfloat16), "dp", scatter_dimension=1, tiled=True
        ).astype(jnp.float32),
        lax.psum_scatter(
            gate_grad.astype(jnp.bfloat16), "dp", scatter_dimension=0, tiled=True
        ).astype(jnp.float32),
        lax.psum_scatter(
            up_grad.astype(jnp.bfloat16), "dp", scatter_dimension=0, tiled=True
        ).astype(jnp.float32),
        lax.psum_scatter(
            down_grad.astype(jnp.bfloat16), "dp", scatter_dimension=1, tiled=True
        ).astype(jnp.float32),
        lax.psum_scatter(
            table_grad.astype(jnp.bfloat16), "dp", scatter_dimension=0, tiled=True
        ).astype(jnp.float32),
    )
    gathered = (
        lax.all_gather(reduced[0].astype(jnp.bfloat16), "dp", axis=0, tiled=True).astype(
            jnp.float32
        ),
        lax.all_gather(reduced[1].astype(jnp.bfloat16), "dp", axis=0, tiled=True).astype(
            jnp.float32
        ),
        lax.all_gather(reduced[2].astype(jnp.bfloat16), "dp", axis=0, tiled=True).astype(
            jnp.float32
        ),
        lax.all_gather(reduced[3].astype(jnp.bfloat16), "dp", axis=1, tiled=True).astype(
            jnp.float32
        ),
        lax.all_gather(reduced[4].astype(jnp.bfloat16), "dp", axis=0, tiled=True).astype(
            jnp.float32
        ),
        lax.all_gather(reduced[5].astype(jnp.bfloat16), "dp", axis=0, tiled=True).astype(
            jnp.float32
        ),
        lax.all_gather(reduced[6].astype(jnp.bfloat16), "dp", axis=1, tiled=True).astype(
            jnp.float32
        ),
        lax.all_gather(reduced[7].astype(jnp.bfloat16), "dp", axis=0, tiled=True).astype(
            jnp.float32
        ),
    )
    return (
        output,
        input_grad,
        gathered[0],
        gathered[1],
        gathered[2],
        gathered[3],
        gathered[4],
        gathered[5],
        gathered[6],
        gain_attn_grad,
        gain_ffn_grad,
        gathered[7],
    )


def solution(mesh):
    return jax.shard_map(
        shards,
        mesh=mesh,
        in_specs=(
            P("dp", None, None),
            P("dp", None),
            P("dp", None, None),
            P(None, "tensor"),
            P(None, "tensor"),
            P(None, "tensor"),
            P("tensor", None),
            P(None, "tensor"),
            P(None, "tensor"),
            P("tensor", None),
            P(),
            P(),
            P(None, "tensor"),
        ),
        out_specs=(
            P("dp", "tensor", None),
            P("dp", "tensor", None),
            P(None, "tensor"),
            P(None, "tensor"),
            P(None, "tensor"),
            P("tensor", None),
            P(None, "tensor"),
            P(None, "tensor"),
            P("tensor", None),
            P(),
            P(),
            P(None, "tensor"),
        ),
        check_vma=False,
    )
```

profile of v0, /device:TPU:0, one launch (start us, length us, event | category | flops | bytes accessed | tf_op | source)
XLA Modules:
  0.0 1494.6 jit_solution(11549578221789818774)
XLA Ops:
  24.2 23.3 %fusion.1 = f32[524288,8]{0,1:T(8,128)} fusion(f32[32,8]{0,1:T(8,128)S(1)} %copy-done.45, s32[524288]{0:T(1024)S(1)} %fusion.51), kind=kOutput, calls=%fused_computation.2 | convolution fusion | flops 1627389952 | bytes 18875392 | tf_op jit(solution)/shard_map/dot_general | solution.py:105
  49.1 23.8 %fusion.3 = f32[524288,8]{0,1:T(8,128)} fusion(f32[32,8]{0,1:T(8,128)S(1)} %copy-done.45, s32[524288]{0:T(1024)S(1)} %fusion.50), kind=kOutput, calls=%fused_computation.5 | convolution fusion | flops 1627389952 | bytes 18875392 | tf_op jit(solution)/shard_map/dot_general | solution.py:105
  73.6 21.5 %fusion.84 = (f32[8,512]{1,0:T(8,128)S(1)}, f32[8,512,1024]{2,1,0:T(8,128)}) fusion(f32[1,8,512,1024]{3,1,2,0:T(8,128)} %bitcast.182, bf16[1024,8,64]{0,2,1:T(8,128)(2,1)S(1)} %bitcast.183, bf16[1,1024,8,64]{1,3,2,0:T(8,128)(2,1)S(1)} %bitcast.193, pred[512,1024]{1,0:T(8,128)(4,1)S(1)} %get-tuple-element.52), kind=kOutput, calls=%fused_computation.152 | convolution fusion | flops 549449728 | bytes 35667968 | tf_op jit(solution)/shard_map/qhd,khd->hqk/dot_general | solution.py:59
  95.1 7.8 fusion.11
  109.6 21.5 %fusion.85 = (f32[8,512]{1,0:T(8,128)S(1)}, f32[8,512,1024]{2,1,0:T(8,128)}) fusion(f32[1,8,512,1024]{3,1,2,0:T(8,128)} %bitcast.181, bf16[1024,8,64]{0,2,1:T(8,128)(2,1)S(1)} %bitcast.184, bf16[1,1024,8,64]{1,3,2,0:T(8,128)(2,1)S(1)} %bitcast.194, pred[512,1024]{1,0:T(8,128)(4,1)S(1)} %get-tuple-element.51), kind=kOutput, calls=%fused_computation.153 | convolution fusion | flops 549449728 | bytes 35667968 | tf_op jit(solution)/shard_map/qhd,khd->hqk/dot_general | solution.py:59
  131.1 7.8 fusion.10
  151.5 157.4 %all-reduce.7.cloned.1.call-done = bf16[1024,2048]{1,0:T(8,128)(2,1)} async-done(((bf16[1024,2048]{1,0:T(8,128)(2,1)}), bf16[1024,2048]{1,0:T(8,128)(2,1)}) %all-reduce.7.cloned.1.call-update) | async-done | bytes 4194320 | tf_op jit(solution)/shard_map/psum | solution.py:130
  317.7 7.3 fusion.87
  324.9 11.4 multiply_convert_fusion.2
  336.4 13.3 fusion.32
  349.6 7.8 fusion.88
  357.5 11.2 add_convert_fusion.1
  368.8 154.1 %all-reduce.9.cloned.1.call-done = bf16[1024,2048]{1,0:T(8,128)(2,1)} async-done(((bf16[1024,2048]{1,0:T(8,128)(2,1)}), bf16[1024,2048]{1,0:T(8,128)(2,1)}) %all-reduce.9.cloned.1.call-update) | async-done | bytes 4194320 | tf_op jit(solution)/shard_map/psum | solution.py:152
  522.8 6.7 multiply_reduce_fusion.2
  531.1 10.1 multiply_add_fusion
  541.2 6.9 fusion.64
  548.1 13.4 multiply_reduce_fusion.1
  565.7 8.8 add_convert_fusion.2
  580.0 18.7 %fusion.42 = (f32[1,8,512,1024]{3,2,1,0:T(8,128)}, bf16[8,512,1024]{2,1,0:T(8,128)(2,1)S(1)}) fusion(f32[8,512,1024]{2,1,0:T(8,128)} %get-tuple-element.68, f32[8,512]{1,0:T(8,128)S(1)} %get-tuple-element.67, f32[8,512,1024]{2,1,0:T(8,128)} %get-tuple-element.62, f32[8,512]{1,0:T(8,128)S(1)} %log_add_fusion.1), kind=kLoop, calls=%fused_computation.75 | loop fusion | flops 16777216 | bytes 58753024
  602.0 7.1 convolution_convert_fusion.5
  609.1 11.9 multiply_reduce_fusion
  621.0 19.4 %fusion.44 = (f32[1,8,512,1024]{3,2,1,0:T(8,128)}, bf16[8,512,1024]{2,1,0:T(8,128)(2,1)S(1)}) fusion(f32[8,512,1024]{2,1,0:T(8,128)} %get-tuple-element.66, f32[8,512]{1,0:T(8,128)S(1)} %get-tuple-element.65, f32[8,512,1024]{2,1,0:T(8,128)} %get-tuple-element.60, f32[8,512]{1,0:T(8,128)S(1)} %log_add_fusion), kind=kLoop, calls=%fused_computation.77 | loop fusion | flops 16777216 | bytes 58753024
  663.5 10.0 convolution_convert_fusion.2
  673.5 9.9 convolution_convert_fusion.1
  683.5 9.0 fusion.86
  692.6 9.1 fusion.41
  703.2 7.5 convolution_convert_fusion
  712.7 42.1 %reduce-scatter.8.cloned.1.call-done = bf16[256,512]{1,0:T(8,128)(2,1)} async-done(((bf16[2048,512]{1,0:T(8,128)(2,1)}), bf16[256,512]{1,0:T(8,128)(2,1)}) %reduce-scatter.8.cloned.1.call-update) | async-done | bytes 262160 | tf_op jit(solution)/shard_map/reduce_scatter | solution.py:236
  754.9 10.4 convolution_convert_fusion.3
  776.5 38.9 %reduce-scatter.16.cloned.1.call-done = bf16[256,1280]{1,0:T(8,128)(2,1)} async-done(((bf16[2048,1280]{1,0:T(8,128)(2,1)}), bf16[256,1280]{1,0:T(8,128)(2,1)}) %reduce-scatter.16.cloned.1.call-update) | async-done | bytes 655376 | tf_op jit(solution)/shard_map/reduce_scatter | solution.py:248
  815.4 60.3 %reduce-scatter.18.cloned.1.call-done = bf16[256,1280]{1,0:T(8,128)(2,1)} async-done(((bf16[2048,1280]{1,0:T(8,128)(2,1)}), bf16[256,1280]{1,0:T(8,128)(2,1)}) %reduce-scatter.18.cloned.1.call-update) | async-done | bytes 655376 | tf_op jit(solution)/shard_map/reduce_scatter | solution.py:251
  875.8 59.9 %reduce-scatter.20.cloned.1.call-done = bf16[1280,256]{1,0:T(8,128)(2,1)} async-done(((bf16[1280,2048]{1,0:T(8,128)(2,1)}), bf16[1280,256]{1,0:T(8,128)(2,1)}) %reduce-scatter.20.cloned.1.call-update) | async-done | bytes 655376 | tf_op jit(solution)/shard_map/reduce_scatter | solution.py:254
  935.8 6.7 convert_element_type.351
  944.5 18.4 %copy.33 = f32[1,8,512,1024]{3,1,2,0:T(8,128)} copy(f32[1,8,512,1024]{3,2,1,0:T(8,128)} %get-tuple-element.40) | data formatting | bytes 33554432
  962.9 18.1 %copy.34 = f32[1,8,512,1024]{3,1,2,0:T(8,128)} copy(f32[1,8,512,1024]{3,2,1,0:T(8,128)} %get-tuple-element.42) | data formatting | bytes 33554432
  981.0 34.5 %fusion = f32[32,8]{1,0:T(8,128)S(1)} fusion(f32[8,524288]{1,0:T(8,128)} %bitcast.188, s32[524288]{0:T(1024)S(1)} %copy-done.21), kind=kOutput, calls=%fused_computation.1 | convolution fusion | flops 1627389952 | bytes 18875392 | tf_op jit(solution)/shard_map/dot_general | solution.py:212
  1015.5 34.6 %fusion.74 = bf16[32,8]{1,0:T(8,128)(2,1)S(1)} fusion(f32[32,8]{1,0:T(8,128)S(1)} %fusion, f32[8,524288]{1,0:T(8,128)} %bitcast.187, s32[524288]{0:T(1024)S(1)} %copy-done.23), kind=kOutput, calls=%fused_computation.129 | convolution fusion | flops 1627390464 | bytes 18875904 | tf_op jit(solution)/shard_map/dot_general | solution.py:212
  1050.2 12.6 all-reduce
  1062.9 9.7 all-gather
  1096.6 253.2 %all-reduce.11.cloned.1.call-done = (bf16[1024,2048]{1,0:T(8,128)(2,1)}, bf16[1024,2048]{1,0:T(8,128)(2,1)}) async-done(((bf16[1024,2048]{1,0:T(8,128)(2,1)}, bf16[1024,2048]{1,0:T(8,128)(2,1)}), (bf16[1024,2048]{1,0:T(8,128)(2,1)}, bf16[1024,2048]{1,0:T(8,128)(2,1)})) %all-reduce.11.cloned.1.call-update) | async-done | bytes 8388624 | tf_op jit(solution)/shard_map/psum | solution.py:138
  1354.6 7.1 fusion.21
  1361.7 6.8 fusion.56
  1368.6 39.7 %all-reduce.1 = (f32[2048]{0:T(1024)}, f32[2048]{0:T(1024)}) all-reduce(f32[2048]{0:T(1024)S(1)} %get-tuple-element.57, f32[2048]{0:T(1024)S(1)} %get-tuple-element.70), channel_id=1, replica_groups=mesh['dp'=8,'tensor'=4] {'dp','tensor'}, use_global_device_ids=true, to_apply=%region_22.23 | all-reduce | flops 4096 | bytes 32768 | tf_op jit(solution)/shard_map/psum | solution.py:234
  1408.2 7.4 convert_element_type.419
  1415.6 20.0 %all-gather.19.cloned.1.call-done = bf16[2048,1280]{1,0:T(8,128)(2,1)} async-done(((bf16[256,1280]{1,0:T(8,128)(2,1)}), bf16[2048,1280]{1,0:T(8,128)(2,1)}) %all-gather.19.cloned.1.call-update) | async-done | bytes 5242896 | tf_op jit(solution)/shard_map/all_gather | solution.py:277
  1435.6 7.5 convert_element_type.421
  1443.2 36.4 %all-gather.21.cloned.1.call-done = bf16[1280,2048]{1,0:T(8,128)(2,1)} async-done(((bf16[1280,256]{1,0:T(8,128)(2,1)}), bf16[1280,2048]{1,0:T(8,128)(2,1)}) %all-gather.21.cloned.1.call-update) | async-done | bytes 5242896 | tf_op jit(solution)/shard_map/all_gather | solution.py:280
  1479.6 8.0 convert_element_type.423
  (220 shorter events, 129.7 us)
Async XLA Ops:
  7.2 139.4 %copy-start = (bf16[512,2048]{1,0:T(8,128)(2,1)S(1)}, bf16[512,2048]{1,0:T(8,128)(2,1)}, u32[]{:S(2)}) copy-start(bf16[512,2048]{1,0:T(8,128)(2,1)} %param.19) | copy-start | bytes 6291460
  7.2 301.7 %all-reduce.7.cloned.1.call-start = ((), (), s32[]{:S(2)}) async-start(), calls=%async_computation.7 | async-start | bytes 8388608 | tf_op jit(solution)/shard_map/psum | solution.py:130
  13.1 96.5 %copy-start.24 = (bf16[1024,512]{0,1:T(8,128)(2,1)}, bf16[1024,512]{0,1:T(8,128)(2,1)S(1)}, u32[]{:S(2)}) copy-start(bf16[1024,512]{0,1:T(8,128)(2,1)S(1)} %convolution_convert_fusion.10) | copy-start | bytes 3145732
  15.7 93.9 %copy-start.17 = (bf16[1024,512]{0,1:T(8,128)(2,1)}, bf16[1024,512]{0,1:T(8,128)(2,1)S(1)}, u32[]{:S(2)}) copy-start(bf16[1024,512]{0,1:T(8,128)(2,1)S(1)} %convolution_convert_fusion.9) | copy-start | bytes 3145732
  24.2 23.3 %copy-start.20 = (s32[524288]{0:T(1024)}, s32[524288]{0:T(1024)S(1)}, u32[]{:S(2)}) copy-start(s32[524288]{0:T(1024)S(1)} %fusion.51) | copy-start | bytes 6291460
  49.1 23.8 %copy-start.22 = (s32[524288]{0:T(1024)}, s32[524288]{0:T(1024)S(1)}, u32[]{:S(2)}) copy-start(s32[524288]{0:T(1024)S(1)} %fusion.50) | copy-start | bytes 6291460
  73.6 29.4 %copy-start.30 = (bf16[1024,512]{0,1:T(8,128)(2,1)S(1)}, bf16[1024,512]{0,1:T(8,128)(2,1)}, u32[]{:S(2)}) copy-start(bf16[1024,512]{0,1:T(8,128)(2,1)} %convolution_convert_fusion.11) | copy-start | bytes 3145732
  95.1 10.6 copy-start.2
  131.0 10.6 copy-start.3
  151.0 162.9 %copy-start.40 = (f32[2048]{0:T(1024)S(1)}, f32[2048]{0:T(1024)}, u32[]{:S(2)}) copy-start(f32[2048]{0:T(1024)} %param.24) | copy-start | bytes 24580
  151.1 371.8 %all-reduce.9.cloned.1.call-start = ((), (), s32[]{:S(2)}) async-start(), calls=%async_computation.8 | async-start | bytes 8388608 | tf_op jit(solution)/shard_map/psum | solution.py:152
  308.9 8.7 slice-start.4
  314.8 214.8 %copy-start.41 = (f32[1024]{0:T(1024)}, f32[1024]{0:T(1024)S(1)}, u32[]{:S(2)}) copy-start(f32[1024]{0:T(1024)S(1)} %add_rsqrt_fusion) | copy-start | bytes 12292
  317.6 18.7 %copy-start.26 = (bf16[1024,2048]{1,0:T(8,128)(2,1)}, bf16[1024,2048]{1,0:T(8,128)(2,1)S(1)}, u32[]{:S(2)}) copy-start(bf16[1024,2048]{1,0:T(8,128)(2,1)S(1)} %multiply_convert_fusion) | copy-start | bytes 12582916
  317.6 7.3 copy-start.31
  336.4 21.1 %copy-start.54 = (bf16[1024,1280]{1,0:T(8,128)(2,1)}, bf16[1024,1280]{1,0:T(8,128)(2,1)S(1)}, u32[]{:S(2)}) copy-start(bf16[1024,1280]{1,0:T(8,128)(2,1)S(1)} %get-tuple-element.63) | copy-start | bytes 7864324
  349.6 7.9 copy-start.55
  368.7 342.1 %reduce-scatter.12.cloned.1.call-start = ((), (), s32[]{:S(2)}) async-start(), calls=%async_computation.13 | async-start | bytes 2359296 | tf_op jit(solution)/shard_map/reduce_scatter | solution.py:242
  522.8 8.3 copy-start.16
  541.2 20.2 %slice-start = ((s8[16777216]{0:T(1024)(128)(4,1)}), s8[4194304]{0:T(1024)(128)(4,1)S(1)}, s32[]{:S(2)}) async-start(s8[16777216]{0:T(1024)(128)(4,1)} %bitcast.179), calls=%async_computation.24 | async-start | bytes 8388608
  541.2 20.2 %slice-start.1 = ((s8[16777216]{0:T(1024)(128)(4,1)}), s8[4194304]{0:T(1024)(128)(4,1)S(1)}, s32[]{:S(2)}) async-start(s8[16777216]{0:T(1024)(128)(4,1)} %bitcast.179), calls=%async_computation.25 | async-start | bytes 8388608
  548.1 13.4 slice-start.2
  548.1 13.4 slice-start.3
  565.7 9.9 copy-start.7
  565.7 9.9 copy-start.43
  565.7 9.8 copy-start.47
  579.9 131.4 %reduce-scatter.14.cloned.1.call-start = ((), (), s32[]{:S(2)}) async-start(), calls=%async_computation.15 | async-start | bytes 2359296 | tf_op jit(solution)/shard_map/reduce_scatter | solution.py:245
  580.0 18.7 %copy-start.25 = (bf16[1024,512]{0,1:T(8,128)(2,1)S(1)}, bf16[1024,512]{0,1:T(8,128)(2,1)}, u32[]{:S(2)}) copy-start(bf16[1024,512]{0,1:T(8,128)(2,1)} %copy-done.24) | copy-start | bytes 3145732
  621.0 91.1 %reduce-scatter.10.cloned.1.call-start = ((), (), s32[]{:S(2)}) async-start(), calls=%async_computation.11 | async-start | bytes 2359296 | tf_op jit(solution)/shard_map/reduce_scatter | solution.py:239
  650.0 104.8 %reduce-scatter.8.cloned.1.call-start = ((), (), s32[]{:S(2)}) async-start(), calls=%async_computation.9 | async-start | bytes 2359296 | tf_op jit(solution)/shard_map/reduce_scatter | solution.py:236
  663.4 151.9 %reduce-scatter.16.cloned.1.call-start = ((), (), s32[]{:S(2)}) async-start(), calls=%async_computation.17 | async-start | bytes 5898240 | tf_op jit(solution)/shard_map/reduce_scatter | solution.py:248
  673.5 202.2 %reduce-scatter.18.cloned.1.call-start = ((), (), s32[]{:S(2)}) async-start(), calls=%async_computation.19 | async-start | bytes 5898240 | tf_op jit(solution)/shard_map/reduce_scatter | solution.py:251
  683.5 252.3 %reduce-scatter.20.cloned.1.call-start = ((), (), s32[]{:S(2)}) async-start(), calls=%async_computation.21 | async-start | bytes 5898240 | tf_op jit(solution)/shard_map/reduce_scatter | solution.py:254
  683.5 9.1 copy-start.27
  692.6 10.6 copy-start.32
  710.7 369.1 %all-gather.13.cloned.1.call-start = ((), (), s32[]{:S(2)}) async-start(), calls=%async_computation.14 | async-start | bytes 2359296 | tf_op jit(solution)/shard_map/all_gather | solution.py:268
  711.3 372.7 %all-gather.15.cloned.1.call-start = ((), (), s32[]{:S(2)}) async-start(), calls=%async_computation.16 | async-start | bytes 2359296 | tf_op jit(solution)/shard_map/all_gather | solution.py:271
  712.0 376.1 %all-gather.11.cloned.1.call-start = ((), (), s32[]{:S(2)}) async-start(), calls=%async_computation.12 | async-start | bytes 2359296 | tf_op jit(solution)/shard_map/all_gather | solution.py:265
  712.6 379.7 %all-gather.9.cloned.1.call-start = ((), (), s32[]{:S(2)}) async-start(), calls=%async_computation.10 | async-start | bytes 2359296 | tf_op jit(solution)/shard_map/all_gather | solution.py:262
  754.8 10.5 copy-start.34
  754.8 595.0 %all-reduce.11.cloned.1.call-start = ((), (), s32[]{:S(2)}) async-start(), calls=%async_computation.23 | async-start | bytes 16777216 | tf_op jit(solution)/shard_map/psum | solution.py:138
  754.9 10.4 copy-start.49
  776.4 631.8 %all-gather.17.cloned.1.call-start = ((), (), s32[]{:S(2)}) async-start(), calls=%async_computation.18 | async-start | bytes 5898240 | tf_op jit(solution)/shard_map/all_gather | solution.py:274
  815.4 620.2 %all-gather.19.cloned.1.call-start = ((), (), s32[]{:S(2)}) async-start(), calls=%async_computation.20 | async-start | bytes 5898240 | tf_op jit(solution)/shard_map/all_gather | solution.py:277
  875.7 603.9 %all-gather.21.cloned.1.call-start = ((), (), s32[]{:S(2)}) async-start(), calls=%async_computation.22 | async-start | bytes 5898240 | tf_op jit(solution)/shard_map/all_gather | solution.py:280
  962.9 18.1 %copy-start.21 = (s32[524288]{0:T(1024)S(1)}, s32[524288]{0:T(1024)}, u32[]{:S(2)}) copy-start(s32[524288]{0:T(1024)} %copy-done.20) | copy-start | bytes 6291460
  981.0 34.5 %copy-start.23 = (s32[524288]{0:T(1024)S(1)}, s32[524288]{0:T(1024)}, u32[]{:S(2)}) copy-start(s32[524288]{0:T(1024)} %copy-done.22) | copy-start | bytes 6291460
  1435.6 52.0 %copy-start.1 = (bf16[512,2048]{1,0:T(8,128)(2,1)S(1)}, bf16[512,2048]{1,0:T(8,128)(2,1)}, u32[]{:S(2)}) copy-start(bf16[512,2048]{1,0:T(8,128)(2,1)} %param.19) | copy-start | bytes 6291460
  (31 other events, 111.3 us)
Sparse Core Ops, SparseCore 0:
  151.2 157.6 all-reduce.6
  368.8 153.9 all-reduce.8
  580.1 40.2 reduce-scatter.11
  623.8 41.2 reduce-scatter.13
  668.2 41.2 reduce-scatter.9
  713.5 41.2 reduce-scatter.7
  758.7 56.5 reduce-scatter.15
  819.1 56.5 reduce-scatter.17
  879.1 56.5 reduce-scatter.19
  937.6 27.8 all-gather.12
  967.6 28.1 all-gather.14
  997.7 27.8 all-gather.10
  1027.7 27.9 all-gather.8
  1058.3 291.5 all-reduce.10
  1351.7 40.4 all-gather.16
  1394.1 41.4 all-gather.18
  1437.5 42.0 all-gather.20
where the time goes:
time: 1500 us; the launch traced here: 1490 us
  waiting for transfers between devices  824 us (55%)
  matrix products  375 us (25%)
  other arithmetic  155 us (10%)
  blocking collectives  62 us (4%)
  local copies, waits for them, and re-layouts  61.4 us (4%)
  between operations  15.9 us (1%)
    psum x1, waiting for transfers between devices, shards(): lax.psum(ffn_part.astype(jnp.bfloat16), 'tensor').astype(jnp.float32)  253 us
    psum x1, waiting for transfers between devices, shards(): lax.psum(attn_part.astype(jnp.bfloat16), 'tensor').astype(jnp.float32)  157 us
    psum x1, waiting for transfers between devices, shards(): lax.psum(norm_ffn_part.astype(jnp.bfloat16), 'tensor').astype(jnp.float32)  154 us
    dot_general x2, matrix products, shards(): lax.dot_general(onehot, score_sums[block_index].reshape(head_count, block...  69.2 us
    dot_general x9, matrix products, project(): return jnp.dot(left_side, right_side, preferred_element_type=jnp.float32)  62.2 us
    unnamed x133, local copies, waits for them, and re-layouts  60.4 us
    reduce_scatter x1, waiting for transfers between devices, shards(): lax.psum_scatter(up_grad.astype(jnp.bfloat16), 'dp', scatter_dimension=0,...  60.3 us
    reduce_scatter x1, waiting for transfers between devices, shards(): lax.psum_scatter(down_grad.astype(jnp.bfloat16), 'dp', scatter_dimension=...  59.9 us
  transfers between devices with their start and end apart: 17, of which 9 were waited for; matrix products, arithmetic and copies ran while one was open for 21% of the time, Pallas kernels for 0%

commit v1 on v0

--- a/solution.py
+++ b/solution.py
@@ -149,7 +149,9 @@
     gate_grad = weight_term(normed_ffn, grad_gate)
     up_grad = weight_term(normed_ffn, grad_up)
     norm_ffn_part = project_back(grad_gate, w_gate) + project_back(grad_up, w_up)
-    grad_normed_ffn = lax.psum(norm_ffn_part.astype(jnp.bfloat16), "tensor").astype(jnp.float32)
+    grad_normed_ffn = jnp.sum(
+        lax.all_gather(norm_ffn_part.astype(jnp.bfloat16), "tensor"), axis=0
+    ).astype(jnp.float32)
     grad_middle = grad_out.astype(jnp.float32) + norm_back(
         middle, scale_ffn, gain_ffn, grad_normed_ffn
     )

time: 1500 us -> 1630 us (1.087)
  waiting for transfers between devices: 824 us -> 937 us
    all_gather x0 -> x1, waiting for transfers between devices: none -> 237 us  [shards(): lax.all_gather(norm_ffn_part.astype(jnp.bfloat16), 'tensor')]
    psum x1 -> x0, waiting for transfers between devices: 154 us -> none  [shards(): lax.psum(norm_ffn_part.astype(jnp.bfloat16), 'tensor').astype(jnp.float32)]
    reduce_scatter x1, waiting for transfers between devices: 60.3 us -> 0.02 us  [shards(): lax.psum_scatter(up_grad.astype(jnp.bfloat16), 'dp', scatter_dimension=0,...]
    reduce_scatter x1, waiting for transfers between devices: 0.02 us -> 45 us  [shards(): lax.psum_scatter(key_grad.astype(jnp.bfloat16), 'dp', scatter_dimension=0...]
    reduce_scatter x1, waiting for transfers between devices: 0.02 us -> 44.8 us  [shards(): lax.psum_scatter(out_grad.astype(jnp.bfloat16), 'dp', scatter_dimension=1...]
    reduce_scatter x1, waiting for transfers between devices: 0.02 us -> 44.1 us  [shards(): lax.psum_scatter(value_grad.astype(jnp.bfloat16), 'dp', scatter_dimension...]
    reduce_scatter x1, waiting for transfers between devices: 38.9 us -> 0.02 us  [shards(): lax.psum_scatter(gate_grad.astype(jnp.bfloat16), 'dp', scatter_dimension=...]
    reduce_scatter x1, waiting for transfers between devices: 59.9 us -> 24.5 us  [shards(): lax.psum_scatter(down_grad.astype(jnp.bfloat16), 'dp', scatter_dimension=...]
  transfers between devices with their start and end apart: 17 -> 17, of which waited for: 9 -> 11; matrix products, arithmetic and copies ran while one was open for 21% -> 23% of each run, Pallas kernels for 0% -> 0%
where the time goes in v1:
time: 1630 us; the launch traced here: 1620 us
  waiting for transfers between devices  937 us (57%)
  matrix products  370 us (23%)
  other arithmetic  171 us (10%)
  local copies, waits for them, and re-layouts  63.8 us (4%)
  blocking collectives  62 us (4%)
    psum x1, waiting for transfers between devices, shards(): lax.psum(ffn_part.astype(jnp.bfloat16), 'tensor').astype(jnp.float32)  251 us
    all_gather x1, waiting for transfers between devices, shards(): lax.all_gather(norm_ffn_part.astype(jnp.bfloat16), 'tensor')  237 us
    psum x1, waiting for transfers between devices, shards(): lax.psum(attn_part.astype(jnp.bfloat16), 'tensor').astype(jnp.float32)  157 us
    dot_general x2, matrix products, shards(): lax.dot_general(onehot, score_sums[block_index].reshape(head_count, block...  69.1 us
    unnamed x145, local copies, waits for them, and re-layouts  63.5 us
    dot_general x9, matrix products, project(): return jnp.dot(left_side, right_side, preferred_element_type=jnp.float32)  62.1 us
    dot_general x7, matrix products, weight_term(): lax.dot_general(left_side, right_side, (((0,), (0,)), ((), ())), preferre...  47.4 us
    dot_general x7, matrix products, project_back(): lax.dot_general(left_side, right_side, (((1,), (1,)), ((), ())), preferre...  47.4 us
  transfers between devices with their start and end apart: 17, of which 11 were waited for; matrix products, arithmetic and copies ran while one was open for 23% of the time, Pallas kernels for 0%

profile of v1, /device:TPU:0, one launch (start us, length us, event | category | flops | bytes accessed | tf_op | source)
XLA Modules:
  0.0 1621.1 jit_solution(16702438830401462655)
XLA Ops:
  24.2 23.2 %fusion.1 = f32[524288,8]{0,1:T(8,128)} fusion(f32[32,8]{0,1:T(8,128)S(1)} %copy-done.47, s32[524288]{0:T(1024)S(1)} %fusion.51), kind=kOutput, calls=%fused_computation.2 | convolution fusion | flops 1627389952 | bytes 18875392 | tf_op jit(solution)/shard_map/dot_general | solution.py:105
  49.1 23.7 %fusion.3 = f32[524288,8]{0,1:T(8,128)} fusion(f32[32,8]{0,1:T(8,128)S(1)} %copy-done.47, s32[524288]{0:T(1024)S(1)} %fusion.50), kind=kOutput, calls=%fused_computation.5 | convolution fusion | flops 1627389952 | bytes 18875392 | tf_op jit(solution)/shard_map/dot_general | solution.py:105
  73.4 21.5 %fusion.84 = (f32[8,512]{1,0:T(8,128)S(1)}, f32[8,512,1024]{2,1,0:T(8,128)}) fusion(f32[1,8,512,1024]{3,1,2,0:T(8,128)} %bitcast.183, bf16[1024,8,64]{0,2,1:T(8,128)(2,1)S(1)} %bitcast.186, bf16[1,1024,8,64]{1,3,2,0:T(8,128)(2,1)S(1)} %bitcast.197, pred[512,1024]{1,0:T(8,128)(4,1)S(1)} %get-tuple-element.52), kind=kOutput, calls=%fused_computation.152 | convolution fusion | flops 549449728 | bytes 35667968 | tf_op jit(solution)/shard_map/qhd,khd->hqk/dot_general | solution.py:59
  94.9 7.8 fusion.11
  109.4 21.6 %fusion.85 = (f32[8,512]{1,0:T(8,128)S(1)}, f32[8,512,1024]{2,1,0:T(8,128)}) fusion(f32[1,8,512,1024]{3,1,2,0:T(8,128)} %bitcast.182, bf16[1024,8,64]{0,2,1:T(8,128)(2,1)S(1)} %bitcast.187, bf16[1,1024,8,64]{1,3,2,0:T(8,128)(2,1)S(1)} %bitcast.198, pred[512,1024]{1,0:T(8,128)(4,1)S(1)} %get-tuple-element.51), kind=kOutput, calls=%fused_computation.153 | convolution fusion | flops 549449728 | bytes 35667968 | tf_op jit(solution)/shard_map/qhd,khd->hqk/dot_general | solution.py:59
  131.0 7.8 fusion.10
  151.4 157.4 %all-reduce.6.cloned.1.call-done = bf16[1024,2048]{1,0:T(8,128)(2,1)} async-done(((bf16[1024,2048]{1,0:T(8,128)(2,1)}), bf16[1024,2048]{1,0:T(8,128)(2,1)}) %all-reduce.6.cloned.1.call-update) | async-done | bytes 4194320 | tf_op jit(solution)/shard_map/psum | solution.py:130
  317.5 7.3 fusion.87
  324.8 11.4 multiply_convert_fusion.2
  336.3 13.3 fusion.32
  349.5 7.8 fusion.88
  357.4 11.2 add_convert_fusion.1
  368.6 9.8 convolution_convert_fusion.2
  378.5 10.6 convolution_convert_fusion.1
  389.2 9.2 fusion.86
  398.4 9.1 fusion.41
  409.0 7.4 convolution_convert_fusion
  417.2 237.3 %all-gather.25.cloned.1.call-done = bf16[4096,2048]{1,0:T(8,128)(2,1)} async-done(((bf16[1024,2048]{1,0:T(8,128)(2,1)}), bf16[4096,2048]{1,0:T(8,128)(2,1)}) %all-gather.25.cloned.1.call-update) | async-done | bytes 16777232 | tf_op jit(solution)/shard_map/all_gather | solution.py:153
  654.5 12.5 reduce_sum.106
  667.0 7.8 multiply_reduce_fusion.2
  674.9 13.6 multiply_add_fusion
  698.0 8.3 add_convert_fusion.2
  711.6 11.3 multiply_reduce_fusion.1
  723.0 19.4 %fusion.42 = (f32[1,8,512,1024]{3,2,1,0:T(8,128)}, bf16[8,512,1024]{2,1,0:T(8,128)(2,1)S(1)}) fusion(f32[8,512,1024]{2,1,0:T(8,128)} %get-tuple-element.68, f32[8,512]{1,0:T(8,128)S(1)} %get-tuple-element.67, f32[8,512,1024]{2,1,0:T(8,128)} %get-tuple-element.62, f32[8,512]{1,0:T(8,128)S(1)} %log_add_fusion.1), kind=kLoop, calls=%fused_computation.75 | loop fusion | flops 16777216 | bytes 58753024
  747.3 7.1 convolution_convert_fusion.5
  754.5 11.9 multiply_reduce_fusion
  766.4 18.0 %fusion.44 = (f32[1,8,512,1024]{3,2,1,0:T(8,128)}, bf16[8,512,1024]{2,1,0:T(8,128)(2,1)S(1)}) fusion(f32[8,512,1024]{2,1,0:T(8,128)} %get-tuple-element.66, f32[8,512]{1,0:T(8,128)S(1)} %get-tuple-element.65, f32[8,512,1024]{2,1,0:T(8,128)} %get-tuple-element.60, f32[8,512]{1,0:T(8,128)S(1)} %log_add_fusion), kind=kLoop, calls=%fused_computation.77 | loop fusion | flops 16777216 | bytes 58753024
  809.2 24.5 %reduce-scatter.20.cloned.1.call-done = bf16[1280,256]{1,0:T(8,128)(2,1)} async-done(((bf16[1280,2048]{1,0:T(8,128)(2,1)}), bf16[1280,256]{1,0:T(8,128)(2,1)}) %reduce-scatter.20.cloned.1.call-update) | async-done | bytes 655376 | tf_op jit(solution)/shard_map/reduce_scatter | solution.py:256
  834.0 44.1 %reduce-scatter.12.cloned.1.call-done = bf16[256,512]{1,0:T(8,128)(2,1)} async-done(((bf16[2048,512]{1,0:T(8,128)(2,1)}), bf16[256,512]{1,0:T(8,128)(2,1)}) %reduce-scatter.12.cloned.1.call-update) | async-done | bytes 262160 | tf_op jit(solution)/shard_map/reduce_scatter | solution.py:244
  878.2 44.8 %reduce-scatter.14.cloned.1.call-done = bf16[512,256]{1,0:T(8,128)(2,1)} async-done(((bf16[512,2048]{1,0:T(8,128)(2,1)}), bf16[512,256]{1,0:T(8,128)(2,1)}) %reduce-scatter.14.cloned.1.call-update) | async-done | bytes 262160 | tf_op jit(solution)/shard_map/reduce_scatter | solution.py:247
  923.1 45.0 %reduce-scatter.10.cloned.1.call-done = bf16[256,512]{1,0:T(8,128)(2,1)} async-done(((bf16[2048,512]{1,0:T(8,128)(2,1)}), bf16[256,512]{1,0:T(8,128)(2,1)}) %reduce-scatter.10.cloned.1.call-update) | async-done | bytes 262160 | tf_op jit(solution)/shard_map/reduce_scatter | solution.py:241
  968.2 45.4 %reduce-scatter.8.cloned.1.call-done = bf16[256,512]{1,0:T(8,128)(2,1)} async-done(((bf16[2048,512]{1,0:T(8,128)(2,1)}), bf16[256,512]{1,0:T(8,128)(2,1)}) %reduce-scatter.8.cloned.1.call-update) | async-done | bytes 262160 | tf_op jit(solution)/shard_map/reduce_scatter | solution.py:238
  1013.7 10.1 convolution_convert_fusion.3
  1042.8 13.7 all-gather.19.cloned.1.call-done
  1056.5 7.4 convert_element_type.421
  1063.8 35.7 %all-gather.21.cloned.1.call-done = bf16[2048,1280]{1,0:T(8,128)(2,1)} async-done(((bf16[256,1280]{1,0:T(8,128)(2,1)}), bf16[2048,1280]{1,0:T(8,128)(2,1)}) %all-gather.21.cloned.1.call-update) | async-done | bytes 5242896 | tf_op jit(solution)/shard_map/all_gather | solution.py:279
  1099.5 7.4 convert_element_type.423
  1106.9 36.4 %all-gather.23.cloned.1.call-done = bf16[1280,2048]{1,0:T(8,128)(2,1)} async-done(((bf16[1280,256]{1,0:T(8,128)(2,1)}), bf16[1280,2048]{1,0:T(8,128)(2,1)}) %all-gather.23.cloned.1.call-update) | async-done | bytes 5242896 | tf_op jit(solution)/shard_map/all_gather | solution.py:282
  1143.3 8.2 convert_element_type.425
  1156.8 18.6 %copy.33 = f32[1,8,512,1024]{3,1,2,0:T(8,128)} copy(f32[1,8,512,1024]{3,2,1,0:T(8,128)} %get-tuple-element.40) | data formatting | bytes 33554432
  1175.4 20.9 %copy.34 = f32[1,8,512,1024]{3,1,2,0:T(8,128)} copy(f32[1,8,512,1024]{3,2,1,0:T(8,128)S(1)} %bitcast.185) | data formatting | bytes 33554432
  1196.4 34.5 %fusion = f32[32,8]{1,0:T(8,128)S(1)} fusion(f32[8,524288]{1,0:T(8,128)} %bitcast.192, s32[524288]{0:T(1024)S(1)} %copy-done.18), kind=kOutput, calls=%fused_computation.1 | convolution fusion | flops 1627389952 | bytes 18875392 | tf_op jit(solution)/shard_map/dot_general | solution.py:214
  1230.9 34.6 %fusion.74 = bf16[32,8]{1,0:T(8,128)(2,1)S(1)} fusion(f32[32,8]{1,0:T(8,128)S(1)} %fusion, f32[8,524288]{1,0:T(8,128)} %bitcast.191, s32[524288]{0:T(1024)S(1)} %copy-done.20), kind=kOutput, calls=%fused_computation.129 | convolution fusion | flops 1627390464 | bytes 18875904 | tf_op jit(solution)/shard_map/dot_general | solution.py:214
  1265.5 13.8 all-reduce
  1279.3 8.9 all-gather.1
  1305.6 250.9 %all-reduce.8.cloned.1.call-done = (bf16[1024,2048]{1,0:T(8,128)(2,1)}, bf16[1024,2048]{1,0:T(8,128)(2,1)}) async-done(((bf16[1024,2048]{1,0:T(8,128)(2,1)}, bf16[1024,2048]{1,0:T(8,128)(2,1)}), (bf16[1024,2048]{1,0:T(8,128)(2,1)}, bf16[1024,2048]{1,0:T(8,128)(2,1)})) %all-reduce.8.cloned.1.call-update) | async-done | bytes 8388624 | tf_op jit(solution)/shard_map/psum | solution.py:138
  1556.5 10.2 fusion.21
  1574.8 39.4 %all-reduce.1 = (f32[2048]{0:T(1024)}, f32[2048]{0:T(1024)}) all-reduce(f32[2048]{0:T(1024)S(1)} %get-tuple-element.57, f32[2048]{0:T(1024)S(1)} %get-tuple-element.70), channel_id=1, replica_groups=mesh['dp'=8,'tensor'=4] {'dp','tensor'}, use_global_device_ids=true, to_apply=%region_22.23 | all-reduce | flops 4096 | bytes 32768 | tf_op jit(solution)/shard_map/psum | solution.py:236
  (234 shorter events, 143.3 us)
Async XLA Ops:
  7.2 139.3 %copy-start = (bf16[512,2048]{1,0:T(8,128)(2,1)S(1)}, bf16[512,2048]{1,0:T(8,128)(2,1)}, u32[]{:S(2)}) copy-start(bf16[512,2048]{1,0:T(8,128)(2,1)} %param.19) | copy-start | bytes 6291460
  7.2 301.6 %all-reduce.6.cloned.1.call-start = ((), (), s32[]{:S(2)}) async-start(), calls=%async_computation.7 | async-start | bytes 8388608 | tf_op jit(solution)/shard_map/psum | solution.py:130
  13.1 96.3 %copy-start.21 = (bf16[1024,512]{0,1:T(8,128)(2,1)}, bf16[1024,512]{0,1:T(8,128)(2,1)S(1)}, u32[]{:S(2)}) copy-start(bf16[1024,512]{0,1:T(8,128)(2,1)S(1)} %convolution_convert_fusion.10) | copy-start | bytes 3145732
  15.7 93.7 %copy-start.14 = (bf16[1024,512]{0,1:T(8,128)(2,1)}, bf16[1024,512]{0,1:T(8,128)(2,1)S(1)}, u32[]{:S(2)}) copy-start(bf16[1024,512]{0,1:T(8,128)(2,1)S(1)} %convolution_convert_fusion.9) | copy-start | bytes 3145732
  24.2 23.3 %copy-start.17 = (s32[524288]{0:T(1024)}, s32[524288]{0:T(1024)S(1)}, u32[]{:S(2)}) copy-start(s32[524288]{0:T(1024)S(1)} %fusion.51) | copy-start | bytes 6291460
  49.1 23.7 %copy-start.19 = (s32[524288]{0:T(1024)}, s32[524288]{0:T(1024)S(1)}, u32[]{:S(2)}) copy-start(s32[524288]{0:T(1024)S(1)} %fusion.50) | copy-start | bytes 6291460
  73.4 29.4 %copy-start.28 = (bf16[1024,512]{0,1:T(8,128)(2,1)S(1)}, bf16[1024,512]{0,1:T(8,128)(2,1)}, u32[]{:S(2)}) copy-start(bf16[1024,512]{0,1:T(8,128)(2,1)} %convolution_convert_fusion.11) | copy-start | bytes 3145732
  94.9 10.6 copy-start.2
  131.0 10.6 copy-start.3
  150.9 162.9 %copy-start.41 = (f32[2048]{0:T(1024)S(1)}, f32[2048]{0:T(1024)}, u32[]{:S(2)}) copy-start(f32[2048]{0:T(1024)} %param.24) | copy-start | bytes 24580
  150.9 503.6 %all-gather.25.cloned.1.call-start = ((), (), s32[]{:S(2)}) async-start(), calls=%async_computation.22 | async-start | bytes 20971520 | tf_op jit(solution)/shard_map/all_gather | solution.py:153
  308.8 8.7 slice-start.8
  317.5 18.7 %copy-start.24 = (bf16[1024,2048]{1,0:T(8,128)(2,1)}, bf16[1024,2048]{1,0:T(8,128)(2,1)S(1)}, u32[]{:S(2)}) copy-start(bf16[1024,2048]{1,0:T(8,128)(2,1)S(1)} %multiply_convert_fusion) | copy-start | bytes 12582916
  336.2 21.1 %copy-start.56 = (bf16[1024,1280]{1,0:T(8,128)(2,1)}, bf16[1024,1280]{1,0:T(8,128)(2,1)S(1)}, u32[]{:S(2)}) copy-start(bf16[1024,1280]{1,0:T(8,128)(2,1)S(1)} %get-tuple-element.63) | copy-start | bytes 7864324
  368.6 439.4 %reduce-scatter.16.cloned.1.call-start = ((), (), s32[]{:S(2)}) async-start(), calls=%async_computation.16 | async-start | bytes 5898240 | tf_op jit(solution)/shard_map/reduce_scatter | solution.py:250
  378.4 430.1 %reduce-scatter.18.cloned.1.call-start = ((), (), s32[]{:S(2)}) async-start(), calls=%async_computation.18 | async-start | bytes 5898240 | tf_op jit(solution)/shard_map/reduce_scatter | solution.py:253
  389.1 444.6 %reduce-scatter.20.cloned.1.call-start = ((), (), s32[]{:S(2)}) async-start(), calls=%async_computation.20 | async-start | bytes 5898240 | tf_op jit(solution)/shard_map/reduce_scatter | solution.py:256
  389.1 9.3 copy-start.25
  398.4 10.6 copy-start.31
  416.5 461.6 %reduce-scatter.12.cloned.1.call-start = ((), (), s32[]{:S(2)}) async-start(), calls=%async_computation.12 | async-start | bytes 2359296 | tf_op jit(solution)/shard_map/reduce_scatter | solution.py:244
  674.9 19.7 %slice-start = ((s8[16777216]{0:T(1024)(128)(4,1)}), s8[4194304]{0:T(1024)(128)(4,1)S(1)}, s32[]{:S(2)}) async-start(s8[16777216]{0:T(1024)(128)(4,1)} %bitcast.180), calls=%async_computation.24 | async-start | bytes 8388608
  674.9 19.7 %slice-start.1 = ((s8[16777216]{0:T(1024)(128)(4,1)}), s8[4194304]{0:T(1024)(128)(4,1)S(1)}, s32[]{:S(2)}) async-start(s8[16777216]{0:T(1024)(128)(4,1)} %bitcast.180), calls=%async_computation.25 | async-start | bytes 8388608
  674.9 19.7 %slice-start.2 = ((s8[16777216]{0:T(1024)(128)(4,1)}), s8[4194304]{0:T(1024)(128)(4,1)S(1)}, s32[]{:S(2)}) async-start(s8[16777216]{0:T(1024)(128)(4,1)} %bitcast.180), calls=%async_computation.26 | async-start | bytes 8388608
  694.5 17.0 %copy-start.23 = (bf16[1024,512]{0,1:T(8,128)(2,1)}, bf16[1024,512]{0,1:T(8,128)(2,1)S(1)}, u32[]{:S(2)}) copy-start(bf16[1024,512]{0,1:T(8,128)(2,1)S(1)} %fusion.64) | copy-start | bytes 3145732
  698.0 9.4 copy-start.45
  698.0 9.4 copy-start.49
  722.9 200.1 %reduce-scatter.14.cloned.1.call-start = ((), (), s32[]{:S(2)}) async-start(), calls=%async_computation.14 | async-start | bytes 2359296 | tf_op jit(solution)/shard_map/reduce_scatter | solution.py:247
  723.0 22.8 %copy-start.22 = (bf16[1024,512]{0,1:T(8,128)(2,1)S(1)}, bf16[1024,512]{0,1:T(8,128)(2,1)}, u32[]{:S(2)}) copy-start(bf16[1024,512]{0,1:T(8,128)(2,1)} %copy-done.21) | copy-start | bytes 3145732
  766.3 201.7 %reduce-scatter.10.cloned.1.call-start = ((), (), s32[]{:S(2)}) async-start(), calls=%async_computation.10 | async-start | bytes 2359296 | tf_op jit(solution)/shard_map/reduce_scatter | solution.py:241
  794.6 219.0 %reduce-scatter.8.cloned.1.call-start = ((), (), s32[]{:S(2)}) async-start(), calls=%async_computation.8 | async-start | bytes 2359296 | tf_op jit(solution)/shard_map/reduce_scatter | solution.py:238
  807.9 248.6 %all-gather.19.cloned.1.call-start = ((), (), s32[]{:S(2)}) async-start(), calls=%async_computation.17 | async-start | bytes 5898240 | tf_op jit(solution)/shard_map/all_gather | solution.py:276
  808.5 291.0 %all-gather.21.cloned.1.call-start = ((), (), s32[]{:S(2)}) async-start(), calls=%async_computation.19 | async-start | bytes 5898240 | tf_op jit(solution)/shard_map/all_gather | solution.py:279
  809.2 334.1 %all-gather.23.cloned.1.call-start = ((), (), s32[]{:S(2)}) async-start(), calls=%async_computation.21 | async-start | bytes 5898240 | tf_op jit(solution)/shard_map/all_gather | solution.py:282
  833.8 455.1 %all-gather.15.cloned.1.call-start = ((), (), s32[]{:S(2)}) async-start(), calls=%async_computation.13 | async-start | bytes 2359296 | tf_op jit(solution)/shard_map/all_gather | solution.py:270
  878.1 414.9 %all-gather.17.cloned.1.call-start = ((), (), s32[]{:S(2)}) async-start(), calls=%async_computation.15 | async-start | bytes 2359296 | tf_op jit(solution)/shard_map/all_gather | solution.py:273
  923.0 374.2 %all-gather.13.cloned.1.call-start = ((), (), s32[]{:S(2)}) async-start(), calls=%async_computation.11 | async-start | bytes 2359296 | tf_op jit(solution)/shard_map/all_gather | solution.py:267
  968.1 333.3 %all-gather.11.cloned.1.call-start = ((), (), s32[]{:S(2)}) async-start(), calls=%async_computation.9 | async-start | bytes 2359296 | tf_op jit(solution)/shard_map/all_gather | solution.py:264
  1013.6 10.2 copy-start.33
  1013.6 542.8 %all-reduce.8.cloned.1.call-start = ((), (), s32[]{:S(2)}) async-start(), calls=%async_computation.23 | async-start | bytes 16777216 | tf_op jit(solution)/shard_map/psum | solution.py:138
  1013.7 10.1 copy-start.51
  1151.5 23.9 %slice-start.4 = ((s8[16777216]{0:T(1024)(128)(4,1)}), s8[4194304]{0:T(1024)(128)(4,1)S(1)}, s32[]{:S(2)}) async-start(s8[16777216]{0:T(1024)(128)(4,1)} %bitcast.184), calls=%async_computation.28 | async-start | bytes 8388608
  1151.5 23.9 %slice-start.5 = ((s8[16777216]{0:T(1024)(128)(4,1)}), s8[4194304]{0:T(1024)(128)(4,1)S(1)}, s32[]{:S(2)}) async-start(s8[16777216]{0:T(1024)(128)(4,1)} %bitcast.184), calls=%async_computation.29 | async-start | bytes 8388608
  1156.8 18.6 %slice-start.6 = ((s8[16777216]{0:T(1024)(128)(4,1)}), s8[4194304]{0:T(1024)(128)(4,1)S(1)}, s32[]{:S(2)}) async-start(s8[16777216]{0:T(1024)(128)(4,1)} %bitcast.184), calls=%async_computation.30 | async-start | bytes 8388608
  1156.8 18.6 %slice-start.7 = ((s8[16777216]{0:T(1024)(128)(4,1)}), s8[4194304]{0:T(1024)(128)(4,1)S(1)}, s32[]{:S(2)}) async-start(s8[16777216]{0:T(1024)(128)(4,1)} %bitcast.184), calls=%async_computation.31 | async-start | bytes 8388608
  1175.4 21.0 %copy-start.18 = (s32[524288]{0:T(1024)S(1)}, s32[524288]{0:T(1024)}, u32[]{:S(2)}) copy-start(s32[524288]{0:T(1024)} %copy-done.17) | copy-start | bytes 6291460
  1196.4 34.5 %copy-start.20 = (s32[524288]{0:T(1024)S(1)}, s32[524288]{0:T(1024)}, u32[]{:S(2)}) copy-start(s32[524288]{0:T(1024)} %copy-done.19) | copy-start | bytes 6291460
  1556.5 10.2 copy-start.16
  1567.8 46.3 %copy-start.1 = (bf16[512,2048]{1,0:T(8,128)(2,1)S(1)}, bf16[512,2048]{1,0:T(8,128)(2,1)}, u32[]{:S(2)}) copy-start(bf16[512,2048]{1,0:T(8,128)(2,1)} %param.19) | copy-start | bytes 6291460
  (37 other events, 145.4 us)
Sparse Core Ops, SparseCore 0:
  151.0 157.6 all-reduce.5
  368.7 285.7 all-gather.24
  658.9 54.7 reduce-scatter.15
  716.9 56.5 reduce-scatter.17
  777.1 56.5 reduce-scatter.19
  836.9 41.1 reduce-scatter.11
  881.7 41.2 reduce-scatter.13
  926.9 41.1 reduce-scatter.9
  972.3 41.2 reduce-scatter.7
  1015.3 41.1 all-gather.18
  1058.3 41.1 all-gather.20
  1101.2 42.0 all-gather.22
  1145.2 27.8 all-gather.14
  1174.9 28.1 all-gather.16
  1204.8 27.8 all-gather.12
  1234.5 27.8 all-gather.10
  1264.9 291.5 all-reduce.7
